TPU v7x, 32 devices: a whole 2x2x4 slice. The times are simulated.
32 devices in a mesh: grp: 2 (over x), row: 8 (over z, y), col: 2 (over core).
Axes of the slice: x: 2, y: 2, z: 4, core: 2. Of those that a mesh axis runs over, the one named last changes fastest.
Arguments:
- query_window: bfloat16 [16, 8, 128, 1280], P(('grp', 'row'), 'col'), parts along dimension 0, may hold values from -80 to 80
- key_window: bfloat16 [16, 8, 128, 1280], P(('grp', 'row'), 'col'), parts along dimension 0, may hold values from -9 to 9
- value_window: bfloat16 [16, 8, 128, 1280], P(('grp', 'row'), 'col'), parts along dimension 0, may hold values from -6 to 6
- query_index: bfloat16 [16, 8, 128, 1280], P(('grp', 'row'), 'col'), parts along dimension 0, may hold values from -80 to 80
- key_index: bfloat16 [16, 8, 128, 1280], P(('grp', 'row'), 'col'), parts along dimension 0, may hold values from -9 to 9
- proj_weight: bfloat16 [1280, 1024], replicated, may hold values from -0.5 to 0.5
- proj_bias: float32 [1024], replicated, may hold values from -3 to 3
- first_kernel: bfloat16 [3, 3, 256, 256], replicated, may hold values from -0.125 to 0.125
- first_bias: float32 [256], replicated, may hold values from -3 to 3
- second_kernel: bfloat16 [3, 3, 256, 256], replicated, may hold values from -0.125 to 0.125
- second_bias: float32 [256], replicated, may hold values from -3 to 3
Outputs:
- fine_field: bfloat16 [256, 256, 256], P(('grp', 'row'), 'col'), parts along dimension 0
There are 2 independent parts, one for each index of `grp`. A program takes and returns all parts, laid end to end along the dimension named above; an argument that names none is the same for every part. Nothing has to cross between parts.
All inputs are finite; a program needn't handle non-finite values.
Results may differ from a plain program's by a relative error of at most 0.0048.
Values may be sent and summed in bfloat16 or wider, within the bound.
A program may use at most 64 MiB of HBM per device.

v0:
```python
import math
import jax
import jax.numpy as jnp
from jax import lax
from jax.sharding import PartitionSpec as P

HEADS = 8
HEAD_DIM = 160
CHANNELS = 256
TILE_ROWS = 8
TILE_COLS = 16


def extended(value, sides, width):
    for axis, dim in sides:
        size, length = (lax.axis_size(axis), value.shape[dim])
        up = [(i, (i + 1) % size) for i in range(size - 1)]
        down = [(j, i) for i, j in up]
        last = lax.slice_in_dim(value, length - width, length, axis=dim)
        first = lax.slice_in_dim(value, 0, width, axis=dim)
        before = lax.ppermute(last, axis, up)
        after = lax.ppermute(first, axis, down)
        value = jnp.concatenate([before, value, after], axis=dim)
    return value


def softmax_rows(scores):
    highest = jnp.max(scores, axis=-1, keepdims=True)
    raised = jnp.exp(scores - highest)
    return (raised / jnp.sum(raised, axis=-1, keepdims=True)).astype(jnp.bfloat16)


def window_attend(queries, key_rows, values):
    scores = jnp.einsum(
        "blhd,bmhd->bhlm", queries, key_rows, preferred_element_type=jnp.float32
    ) / math.sqrt(HEAD_DIM)
    weights = softmax_rows(scores)
    return jnp.einsum(
        "bhlm,bmhd->blhd", weights, values, preferred_element_type=jnp.float32
    ).astype(jnp.bfloat16)


def index_attend(queries, key_rows, values):
    scores = jnp.einsum(
        "lbhd,mbhd->bhlm", queries, key_rows, preferred_element_type=jnp.float32
    ) / math.sqrt(HEAD_DIM)
    weights = softmax_rows(scores)
    return jnp.einsum(
        "bhlm,mbhd->lbhd", weights, values, preferred_element_type=jnp.float32
    ).astype(jnp.bfloat16)


def convolve(image, kernel, bias):
    height, breadth, depth = image.shape
    padded = extended(image, (("row", 0), ("col", 1)), 1)
    total = jnp.zeros((height * breadth, kernel.shape[-1]), jnp.float32)
    for row_shift in range(3):
        for col_shift in range(3):
            cells = padded[row_shift : row_shift + height, col_shift : col_shift + breadth].reshape(
                -1, depth
            )
            total = total + jnp.dot(
                cells, kernel[row_shift, col_shift], preferred_element_type=jnp.float32
            )
    return (total + bias).reshape(height, breadth, -1)


def shards(
    query_window,
    key_window,
    value_window,
    query_index,
    key_index,
    proj_weight,
    proj_bias,
    first_kernel,
    first_bias,
    second_kernel,
    second_bias,
):
    rows_dev, cols_dev, tokens_win, features = query_window.shape
    layout = (rows_dev * cols_dev, tokens_win, HEADS, HEAD_DIM)
    window_out = window_attend(
        query_window.reshape(layout), key_window.reshape(layout), value_window.reshape(layout)
    ).reshape(query_window.shape)
    count_row = lax.axis_size("row")
    count_col = lax.axis_size("col")
    owned_tokens = tokens_win // (count_row * count_col)
    moved = (
        lax.all_to_all(query_index, ("row", "col"), split_axis=2, concat_axis=0, tiled=True),
        lax.all_to_all(key_index, ("row", "col"), split_axis=2, concat_axis=0, tiled=True),
        lax.all_to_all(window_out, ("row", "col"), split_axis=2, concat_axis=0, tiled=True),
    )
    owner_shape = moved[0].shape
    across = (-1, owned_tokens, HEADS, HEAD_DIM)
    index_out = index_attend(
        moved[0].reshape(across), moved[1].reshape(across), moved[2].reshape(across)
    )
    index_rows = index_out.reshape(-1, features)
    owner_rows = (
        jnp.dot(index_rows, proj_weight, preferred_element_type=jnp.float32) + proj_bias
    ).astype(jnp.bfloat16)
    last = owner_rows.shape[-1]
    shaped = owner_rows.reshape(tuple(owner_shape[:-1]) + (last,))
    returned = lax.all_to_all(shaped, ("row", "col"), split_axis=0, concat_axis=2, tiled=True)
    projected = returned.reshape(rows_dev * cols_dev * tokens_win, last)
    grouped = projected.reshape(rows_dev, cols_dev, TILE_ROWS, TILE_COLS, 2, 2, CHANNELS)
    shuffled = jnp.transpose(grouped, (0, 2, 4, 1, 3, 5, 6)).reshape(
        rows_dev * TILE_ROWS * 2, cols_dev * TILE_COLS * 2, CHANNELS
    )
    activated = jax.nn.gelu(convolve(shuffled, first_kernel, first_bias)).astype(jnp.bfloat16)
    return convolve(activated, second_kernel, second_bias).astype(jnp.bfloat16)


def solution(mesh):
    in_specs = (
        P(("grp", "row"), "col", None, None),
        P(("grp", "row"), "col", None, None),
        P(("grp", "row"), "col", None, None),
        P(("grp", "row"), "col", None, None),
        P(("grp", "row"), "col", None, None),
        P(),
        P(),
        P(),
        P(),
        P(),
        P(),
    )
    out_specs = P(("grp", "row"), "col", None)
    return jax.shard_map(shards, mesh=mesh, in_specs=in_specs, out_specs=out_specs, check_vma=False)
```

profile of v0, /device:TPU:9, one launch (start us, length us, event | category | flops | bytes accessed | tf_op | source)
XLA Modules:
  0.0 240.3 jit_solution(4875045535725694193)
XLA Ops:
  11.8 3.9 %convolution_convert_fusion = bf16[4,8,128,160]{2,3,1,0:T(8,128)(2,1)} fusion(bf16[4,128,8,160]{1,3,2,0:T(8,128)(2,1)} %bitcast.160, f32[4,8,128]{2,1,0:T(8,128)S(1)} %fusion.112, f32[4,8,128,128]{2,3,1,0:T(8,128)} %copy-done.4), kind=kOutput, calls=%fused_computation.58 | convolution fusion | flops 170528896 | bytes 4734976 | tf_op jit(solution)/shard_map/bhlm,bmhd->blhd/dot_general | solution.py:38
  15.7 3.7 %copy.37 = bf16[1,4,128,1280]{3,1,0,2:T(4,128)(2,1)} copy(bf16[1,4,128,1280]{2,3,1,0:T(8,128)(2,1)} %bitcast.161) | data formatting | bytes 2621440 | tf_op jit(solution)/shard_map/reshape | solution.py:85
  19.4 6.6 %all-to-all-start = ((bf16[1,4,128,1280]{3,1,0,2:T(4,128)(2,1)}), bf16[1,4,128,1280]{3,1,0,2:T(4,128)(2,1)}, u32[]{:S(2)}, u32[]{:S(2)}) async-start(bf16[1,4,128,1280]{3,1,0,2:T(4,128)(2,1)} %copy.37), calls=%async_computation | async-start | bytes 2621440 | tf_op jit(solution)/shard_map/all_to_all | solution.py:92
  26.0 3.4 %copy.42 = bf16[1,4,128,1280]{3,1,0,2:T(4,128)(2,1)} copy(bf16[1,4,128,1280]{3,2,1,0:T(8,128)(2,1)} %param.15) | data formatting | bytes 2621440 | tf_op args[4]
  29.4 27.0 %all-to-all-done = bf16[1,4,128,1280]{3,1,0,2:T(4,128)(2,1)} async-done(((bf16[1,4,128,1280]{3,1,0,2:T(4,128)(2,1)}), bf16[1,4,128,1280]{3,1,0,2:T(4,128)(2,1)}, u32[]{:S(2)}, u32[]{:S(2)}) %all-to-all-start) | async-done | bytes 1310752 | tf_op jit(solution)/shard_map/all_to_all | solution.py:92
  56.4 5.0 %all-to-all-start.2 = ((bf16[1,4,128,1280]{3,1,0,2:T(4,128)(2,1)}), bf16[1,4,128,1280]{3,1,0,2:T(4,128)(2,1)}, u32[]{:S(2)}, u32[]{:S(2)}) async-start(bf16[1,4,128,1280]{3,1,0,2:T(4,128)(2,1)} %copy.42), calls=%async_computation.2 | async-start | bytes 2621440 | tf_op jit(solution)/shard_map/all_to_all | solution.py:91
  61.4 3.4 %copy.40 = bf16[1,4,128,1280]{3,1,0,2:T(4,128)(2,1)} copy(bf16[1,4,128,1280]{3,2,1,0:T(8,128)(2,1)} %param.14) | data formatting | bytes 2621440 | tf_op args[3]
  64.8 27.0 %all-to-all-done.2 = bf16[1,4,128,1280]{3,1,0,2:T(4,128)(2,1)} async-done(((bf16[1,4,128,1280]{3,1,0,2:T(4,128)(2,1)}), bf16[1,4,128,1280]{3,1,0,2:T(4,128)(2,1)}, u32[]{:S(2)}, u32[]{:S(2)}) %all-to-all-start.2) | async-done | bytes 1310752 | tf_op jit(solution)/shard_map/all_to_all | solution.py:91
  91.8 5.0 %all-to-all-start.1 = ((bf16[1,4,128,1280]{3,1,0,2:T(4,128)(2,1)}), bf16[1,4,128,1280]{3,1,0,2:T(4,128)(2,1)}, u32[]{:S(2)}, u32[]{:S(2)}) async-start(bf16[1,4,128,1280]{3,1,0,2:T(4,128)(2,1)} %copy.40), calls=%async_computation.1 | async-start | bytes 2621440 | tf_op jit(solution)/shard_map/all_to_all | solution.py:90
  99.5 4.8 %reshape.99 = bf16[64,8,8,160]{3,2,1,0:T(8,128)(2,1)} reshape(bf16[16,1,4,8,1280]{4,3,2,0,1:T(8,128)(2,1)} %copy.39) | data formatting | bytes 2621440 | tf_op jit(solution)/shard_map/reshape | solution.py:97
  106.9 4.8 %reshape.101 = bf16[64,8,8,160]{3,2,1,0:T(8,128)(2,1)} reshape(bf16[16,1,4,8,1280]{4,3,2,0,1:T(8,128)(2,1)} %bitcast.140) | data formatting | bytes 2621440 | tf_op jit(solution)/shard_map/reshape | solution.py:97
  111.7 15.5 %all-to-all-done.1 = bf16[1,4,128,1280]{3,1,0,2:T(4,128)(2,1)} async-done(((bf16[1,4,128,1280]{3,1,0,2:T(4,128)(2,1)}), bf16[1,4,128,1280]{3,1,0,2:T(4,128)(2,1)}, u32[]{:S(2)}, u32[]{:S(2)}) %all-to-all-start.1) | async-done | bytes 1310752 | tf_op jit(solution)/shard_map/all_to_all | solution.py:90
  129.7 4.8 %reshape.100 = bf16[64,8,8,160]{3,2,1,0:T(8,128)(2,1)} reshape(bf16[16,1,4,8,1280]{4,3,2,0,1:T(8,128)(2,1)} %bitcast.141) | data formatting | bytes 2621440 | tf_op jit(solution)/shard_map/reshape | solution.py:97
  134.6 4.6 %fusion.26 = f32[8,8,64,64]{2,3,1,0:T(8,128)S(1)} fusion(bf16[64,8,8,160]{3,2,1,0:T(8,128)(2,1)} %reshape.101, bf16[64,8,8,160]{3,2,1,0:T(8,128)(2,1)} %reshape.100), kind=kOutput, calls=%fused_computation.41 | convolution fusion | flops 83886080 | bytes 3670016 | tf_op jit(solution)/shard_map/lbhd,mbhd->bhlm/dot_general | solution.py:44
  141.2 5.6 %convert_bitcast_fusion = bf16[64,8,8,160]{3,0,2,1:T(8,128)(2,1)} fusion(bf16[64,8,8,160]{3,2,1,0:T(8,128)(2,1)} %reshape.99, f32[8,8,64]{2,1,0:T(8,128)S(1)} %fusion.113, f32[8,8,64,64]{2,3,1,0:T(8,128)} %copy-done.3), kind=kOutput, calls=%fused_computation.45 | convolution fusion | flops 85594176 | bytes 3686400 | tf_op jit(solution)/shard_map/bhlm,mbhd->lbhd/dot_general | solution.py:48
  146.8 4.1 %copy.48 = bf16[64,8,8,160]{3,2,1,0:T(8,128)(2,1)} copy(bf16[64,8,8,160]{3,0,2,1:T(8,128)(2,1)} %convert_bitcast_fusion) | data formatting | bytes 2621440 | tf_op jit(solution)/shard_map/convert_element_type | solution.py:50
  150.9 4.6 %reshape.102 = bf16[512,1280]{1,0:T(8,128)(2,1)} reshape(bf16[64,8,8,160]{3,2,1,0:T(8,128)(2,1)} %copy.48) | data formatting | bytes 2621440 | tf_op jit(solution)/shard_map/reshape | solution.py:99
  158.4 30.2 %all_to_all.60 = bf16[16,4,8,1024]{3,2,1,0:T(8,128)(2,1)S(1)} all-to-all(bf16[16,4,8,1024]{3,2,1,0:T(8,128)(2,1)S(1)} %bitcast.162), channel_id=1, replica_groups=mesh['grp'=2,'row'=8,'col'=2] {'row','col'}, dimensions={0} | all-to-all | bytes 2097152 | tf_op jit(solution)/shard_map/all_to_all | solution.py:105
  196.8 3.6 %collective-permute-start.1 = (bf16[1,128,256]{2,1,0:T(8,128)(2,1)S(1)}, bf16[1,128,256]{2,1,0:T(8,128)(2,1)S(1)}, u32[]{:S(2)}, u32[]{:S(2)}) collective-permute-start(bf16[1,128,256]{2,1,0:T(8,128)(2,1)S(1)} %get-tuple-element.33), channel_id=1, source_target_pairs={{2,0},{4,2},{6,4},{8,6},{10,8},{12,10},{14,12},{3,1},{5,3},{7,5},{... | collective-permute-start | bytes 196616 | tf_op jit(solution)/shard_map/ppermute | solution.py:22
  203.5 3.5 %collective-permute-start.3 = (bf16[18,1,256]{2,1,0:T(2,128)(2,1)S(1)}, bf16[18,1,256]{2,1,0:T(2,128)(2,1)S(1)}, u32[]{:S(2)}, u32[]{:S(2)}) collective-permute-start(bf16[18,1,256]{2,1,0:T(2,128)(2,1)S(1)} %get-tuple-element.25), channel_id=1, source_target_pairs={{1,0},{3,2},{5,4},{7,6},{9,8},{11,10},{13,12},{15,14},{17,16},{19,... | collective-permute-start | bytes 27656 | tf_op jit(solution)/shard_map/ppermute | solution.py:22
  207.8 3.7 %pad_maximum_fusion.5 = (bf16[16,128,256]{2,1,0:T(8,128)(2,1)S(1)}, bf16[16,128,256]{2,1,0:T(8,128)(2,1)S(1)}, bf16[16,128,256]{2,1,0:T(8,128)(2,1)S(1)}, bf16[1...) fusion(bf16[18,128,256]{2,1,0:T(8,128)(2,1)S(1)} %constant_dynamic-update-slice_, ...), kind=kLoop, calls=%fused_computation.76 | loop fusion | flops 12582912 | bytes 7489536 | tf_op jit(solution)/shard_map/concatenate | solution.py:23
  216.5 4.6 %collective-permute-start.5 = (bf16[1,128,256]{2,1,0:T(8,128)(2,1)S(1)}, bf16[1,128,256]{2,1,0:T(8,128)(2,1)S(1)}, u32[]{:S(2)}, u32[]{:S(2)}) collective-permute-start(bf16[1,128,256]{2,1,0:T(8,128)(2,1)S(1)} %get-tuple-element.29), channel_id=1, source_target_pairs={{2,0},{4,2},{6,4},{8,6},{10,8},{12,10},{14,12},{3,1},{5,3},{7,5},{... | collective-permute-start | bytes 196616 | tf_op jit(solution)/shard_map/ppermute | solution.py:22
  223.3 3.9 %collective-permute-done.4 = bf16[1,128,256]{2,1,0:T(8,128)(2,1)S(1)} collective-permute-done((bf16[1,128,256]{2,1,0:T(8,128)(2,1)S(1)}, bf16[1,128,256]{2,1,0:T(8,128)(2,1)S(1)}, u32[]{:S(2)}, u32[]{:S(2)}) %collective-permute-start.4) | collective-permute-done | bytes 65568 | tf_op jit(solution)/shard_map/ppermute | solution.py:21
  228.5 3.9 %collective-permute-start.7 = (bf16[18,1,256]{2,1,0:T(2,128)(2,1)S(1)}, bf16[18,1,256]{2,1,0:T(2,128)(2,1)S(1)}, u32[]{:S(2)}, u32[]{:S(2)}) collective-permute-start(bf16[18,1,256]{2,1,0:T(2,128)(2,1)S(1)} %get-tuple-element.20), channel_id=1, source_target_pairs={{1,0},{3,2},{5,4},{7,6},{9,8},{11,10},{13,12},{15,14},{17,16},{19,... | collective-permute-start | bytes 27656 | tf_op jit(solution)/shard_map/ppermute | solution.py:22
  (76 shorter events, 52.7 us)
Async XLA Ops:
  0.0 155.5 %copy-start = (bf16[1280,1024]{1,0:T(8,128)(2,1)S(1)}, bf16[1280,1024]{1,0:T(8,128)(2,1)}, u32[]{:S(2)}) copy-start(bf16[1280,1024]{1,0:T(8,128)(2,1)} %param.16) | copy-start | bytes 7864324
  9.9 1.3 copy-start.4
  19.4 37.0 %all-to-all-start = ((bf16[1,4,128,1280]{3,1,0,2:T(4,128)(2,1)}), bf16[1,4,128,1280]{3,1,0,2:T(4,128)(2,1)}, u32[]{:S(2)}, u32[]{:S(2)}) async-start(bf16[1,4,128,1280]{3,1,0,2:T(4,128)(2,1)} %copy.37), calls=%async_computation | async-start | bytes 2621440 | tf_op jit(solution)/shard_map/all_to_all | solution.py:92
  56.4 35.4 %all-to-all-start.2 = ((bf16[1,4,128,1280]{3,1,0,2:T(4,128)(2,1)}), bf16[1,4,128,1280]{3,1,0,2:T(4,128)(2,1)}, u32[]{:S(2)}, u32[]{:S(2)}) async-start(bf16[1,4,128,1280]{3,1,0,2:T(4,128)(2,1)} %copy.42), calls=%async_computation.2 | async-start | bytes 2621440 | tf_op jit(solution)/shard_map/all_to_all | solution.py:91
  91.8 35.4 %all-to-all-start.1 = ((bf16[1,4,128,1280]{3,1,0,2:T(4,128)(2,1)}), bf16[1,4,128,1280]{3,1,0,2:T(4,128)(2,1)}, u32[]{:S(2)}, u32[]{:S(2)}) async-start(bf16[1,4,128,1280]{3,1,0,2:T(4,128)(2,1)} %copy.40), calls=%async_computation.1 | async-start | bytes 2621440 | tf_op jit(solution)/shard_map/all_to_all | solution.py:90
  139.2 1.3 copy-start.3
  150.9 4.6 %copy-start.9 = (f32[1024]{0:T(1024)S(1)}, f32[1024]{0:T(1024)}, u32[]{:S(2)}) copy-start(f32[1024]{0:T(1024)} %param.17) | copy-start | bytes 12292
  193.1 7.4 %collective-permute-start = (bf16[1,128,256]{2,1,0:T(8,128)(2,1)S(1)}, bf16[1,128,256]{2,1,0:T(8,128)(2,1)S(1)}, u32[]{:S(2)}, u32[]{:S(2)}) collective-permute-start(bf16[1,128,256]{2,1,0:T(8,128)(2,1)S(1)} %get-tuple-element.34), channel_id=1, source_target_pairs={{0,2},{2,4},{4,6},{6,8},{8,10},{10,12},{12,14},{1,3},{3,5},{5,7},{... | collective-permute-start | bytes 196616 | tf_op jit(solution)/shard_map/ppermute | solution.py:21
  196.8 5.0 %collective-permute-start.1 = (bf16[1,128,256]{2,1,0:T(8,128)(2,1)S(1)}, bf16[1,128,256]{2,1,0:T(8,128)(2,1)S(1)}, u32[]{:S(2)}, u32[]{:S(2)}) collective-permute-start(bf16[1,128,256]{2,1,0:T(8,128)(2,1)S(1)} %get-tuple-element.33), channel_id=1, source_target_pairs={{2,0},{4,2},{6,4},{8,6},{10,8},{12,10},{14,12},{3,1},{5,3},{7,5},{... | collective-permute-start | bytes 196616 | tf_op jit(solution)/shard_map/ppermute | solution.py:22
  200.5 6.5 %copy-start.5 = (bf16[3,3,256,256]{3,2,1,0:T(8,128)(2,1)S(1)}, bf16[3,3,256,256]{3,2,1,0:T(8,128)(2,1)}, u32[]{:S(2)}) copy-start(bf16[3,3,256,256]{3,2,1,0:T(8,128)(2,1)} %param.18) | copy-start | bytes 3538948
  202.2 5.6 %collective-permute-start.2 = (bf16[18,1,256]{2,1,0:T(2,128)(2,1)S(1)}, bf16[18,1,256]{2,1,0:T(2,128)(2,1)S(1)}, u32[]{:S(2)}, u32[]{:S(2)}) collective-permute-start(bf16[18,1,256]{2,1,0:T(2,128)(2,1)S(1)} %get-tuple-element.24), channel_id=1, source_target_pairs={{0,1},{2,3},{4,5},{6,7},{8,9},{10,11},{12,13},{14,15},{16,17},{18,... | collective-permute-start | bytes 27656 | tf_op jit(solution)/shard_map/ppermute | solution.py:21
  203.5 4.4 %collective-permute-start.3 = (bf16[18,1,256]{2,1,0:T(2,128)(2,1)S(1)}, bf16[18,1,256]{2,1,0:T(2,128)(2,1)S(1)}, u32[]{:S(2)}, u32[]{:S(2)}) collective-permute-start(bf16[18,1,256]{2,1,0:T(2,128)(2,1)S(1)} %get-tuple-element.25), channel_id=1, source_target_pairs={{1,0},{3,2},{5,4},{7,6},{9,8},{11,10},{13,12},{15,14},{17,16},{19,... | collective-permute-start | bytes 27656 | tf_op jit(solution)/shard_map/ppermute | solution.py:22
  212.8 1.2 copy-start.2
  214.5 0.7 copy-start.7
  216.5 6.8 %collective-permute-start.5 = (bf16[1,128,256]{2,1,0:T(8,128)(2,1)S(1)}, bf16[1,128,256]{2,1,0:T(8,128)(2,1)S(1)}, u32[]{:S(2)}, u32[]{:S(2)}) collective-permute-start(bf16[1,128,256]{2,1,0:T(8,128)(2,1)S(1)} %get-tuple-element.29), channel_id=1, source_target_pairs={{2,0},{4,2},{6,4},{8,6},{10,8},{12,10},{14,12},{3,1},{5,3},{7,5},{... | collective-permute-start | bytes 196616 | tf_op jit(solution)/shard_map/ppermute | solution.py:22
  221.1 11.4 %copy-start.6 = (bf16[3,3,256,256]{3,2,1,0:T(8,128)(2,1)S(1)}, bf16[3,3,256,256]{3,2,1,0:T(8,128)(2,1)}, u32[]{:S(2)}) copy-start(bf16[3,3,256,256]{3,2,1,0:T(8,128)(2,1)} %param.20) | copy-start | bytes 3538948
  221.1 6.0 %collective-permute-start.4 = (bf16[1,128,256]{2,1,0:T(8,128)(2,1)S(1)}, bf16[1,128,256]{2,1,0:T(8,128)(2,1)S(1)}, u32[]{:S(2)}, u32[]{:S(2)}) collective-permute-start(bf16[1,128,256]{2,1,0:T(8,128)(2,1)S(1)} %get-tuple-element.28), channel_id=1, source_target_pairs={{0,2},{2,4},{4,6},{6,8},{8,10},{10,12},{12,14},{1,3},{3,5},{5,7},{... | collective-permute-start | bytes 196616 | tf_op jit(solution)/shard_map/ppermute | solution.py:21
  227.2 5.8 %collective-permute-start.6 = (bf16[18,1,256]{2,1,0:T(2,128)(2,1)S(1)}, bf16[18,1,256]{2,1,0:T(2,128)(2,1)S(1)}, u32[]{:S(2)}, u32[]{:S(2)}) collective-permute-start(bf16[18,1,256]{2,1,0:T(2,128)(2,1)S(1)} %get-tuple-element.19), channel_id=1, source_target_pairs={{0,1},{2,3},{4,5},{6,7},{8,9},{10,11},{12,13},{14,15},{16,17},{18,... | collective-permute-start | bytes 27656 | tf_op jit(solution)/shard_map/ppermute | solution.py:21
  228.5 4.5 %collective-permute-start.7 = (bf16[18,1,256]{2,1,0:T(2,128)(2,1)S(1)}, bf16[18,1,256]{2,1,0:T(2,128)(2,1)S(1)}, u32[]{:S(2)}, u32[]{:S(2)}) collective-permute-start(bf16[18,1,256]{2,1,0:T(2,128)(2,1)S(1)} %get-tuple-element.20), channel_id=1, source_target_pairs={{1,0},{3,2},{5,4},{7,6},{9,8},{11,10},{13,12},{15,14},{17,16},{19,... | collective-permute-start | bytes 27656 | tf_op jit(solution)/shard_map/ppermute | solution.py:22
  238.0 0.7 copy-start.8
  238.4 1.9 copy-start.1
where the time goes:
time: 242 us; the launch traced here: 240 us
  waiting for transfers between devices  74.8 us (31%)
  local copies, waits for them, and re-layouts  59.8 us (25%)
  starting transfers between devices  39.4 us (16%)
  blocking collectives  30.2 us (12%)
  matrix products  29 us (12%)
  other arithmetic  6.82 us (3%)
    all_to_all x1, blocking collectives, shards(): lax.all_to_all(shaped, ('row', 'col'), split_axis=0, concat_axis=2, tiled...  30.2 us
    all_to_all x1, waiting for transfers between devices, shards(): lax.all_to_all(key_index, ('row', 'col'), split_axis=2, concat_axis=0, ti...  27 us
    all_to_all x1, waiting for transfers between devices, shards(): lax.all_to_all(window_out, ('row', 'col'), split_axis=2, concat_axis=0, t...  27 us
    unnamed x26, local copies, waits for them, and re-layouts  18.4 us
    ppermute x4, starting transfers between devices, extended(): after = lax.ppermute(first, axis, down)  15.6 us
    all_to_all x1, waiting for transfers between devices, shards(): lax.all_to_all(query_index, ('row', 'col'), split_axis=2, concat_axis=0,...  15.5 us
    dot_general x18, matrix products, convolve(): jnp.dot(cells, kernel[row_shift, col_shift], preferred_element_type=jnp.f...  9.53 us
    ppermute x4, starting transfers between devices, extended(): before = lax.ppermute(last, axis, up)  7.18 us
  transfers between devices with their start and end apart: 11, of which 6 were waited for; matrix products, arithmetic and copies ran while one was open for 10% of the time, Pallas kernels for 0%

commit v1 on v0

--- a/solution.py
+++ b/solution.py
@@ -9,6 +9,29 @@
 CHANNELS = 256
 TILE_ROWS = 8
 TILE_COLS = 16
+
+
+def split_up(array, dim, size):
+    before, after = (array.shape[:dim], array.shape[dim + 1 :])
+    return jnp.moveaxis(array.reshape(*before, size, -1, *after), dim, 0)
+
+
+def in_order(blocks, dim):
+    blocks = jnp.moveaxis(blocks, 0, dim)
+    shape = blocks.shape
+    return blocks.reshape(*shape[:dim], shape[dim] * shape[dim + 1], *shape[dim + 2 :])
+
+
+def exchange_directly(array, axis, split_dim, concat_dim):
+    size, place = (lax.axis_size(axis), lax.axis_index(axis))
+    blocks = split_up(array, split_dim, size)
+    result = blocks
+    for step in range(1, size):
+        target, source = ((place + step) % size, (place - step) % size)
+        sent = lax.dynamic_index_in_dim(blocks, target, 0)
+        theirs = lax.ppermute(sent, axis, [(i, (i + step) % size) for i in range(size)])
+        result = lax.dynamic_update_slice_in_dim(result, theirs, source, axis=0)
+    return in_order(result, concat_dim)
 
 
 def extended(value, sides, width):
@@ -89,7 +112,7 @@
     moved = (
         lax.all_to_all(query_index, ("row", "col"), split_axis=2, concat_axis=0, tiled=True),
         lax.all_to_all(key_index, ("row", "col"), split_axis=2, concat_axis=0, tiled=True),
-        lax.all_to_all(window_out, ("row", "col"), split_axis=2, concat_axis=0, tiled=True),
+        exchange_directly(window_out, ("row", "col"), 2, 0),
     )
     owner_shape = moved[0].shape
     across = (-1, owned_tokens, HEADS, HEAD_DIM)

time: 242 us -> 237 us (0.979)
  waiting for transfers between devices: 74.8 us -> 26.8 us
  local copies, waits for them, and re-layouts: 59.8 us -> 84.8 us
  starting transfers between devices: 39.4 us -> 54.4 us
  blocking collectives: 30.2 us -> 33.4 us
    all_to_all x1, waiting for transfers between devices: 27 us -> 0.01 us  [shards(): lax.all_to_all(key_index, ('row', 'col'), split_axis=2, concat_axis=0, ti...]
    all_to_all x1 -> x0, waiting for transfers between devices: 27 us -> none  [shards(): lax.all_to_all(window_out, ('row', 'col'), split_axis=2, concat_axis=0, t...]
    ppermute x0 -> x15, waiting for transfers between devices: none -> 21.5 us  [exchange_directly(): lax.ppermute(sent, axis, [(i, (i + step) % size) for i in range(size)])]
    ppermute x0 -> x15, starting transfers between devices: none -> 20.9 us  [exchange_directly(): lax.ppermute(sent, axis, [(i, (i + step) % size) for i in range(size)])]
    dynamic_update_slice x0 -> x16, local copies, waits for them, and re-layouts: none -> 20.3 us  [exchange_directly(): result = lax.dynamic_update_slice_in_dim(result, theirs, source, axis=0)]
    all_to_all x1, waiting for transfers between devices: 15.5 us -> 0.01 us  [shards(): lax.all_to_all(query_index, ('row', 'col'), split_axis=2, concat_axis=0,...]
    another operation x0 -> x2, local copies, waits for them, and re-layouts: none -> 9.41 us  [the longest x1 4.84 us: shards(): moved[2].reshape(across)]
    reshape x2 -> x0, local copies, waits for them, and re-layouts: 8.54 us -> none  [the longest x1 4.85 us: shards(): moved[2].reshape(across)]
  transfers between devices with their start and end apart: 11 -> 25, of which waited for: 6 -> 6; matrix products, arithmetic and copies ran while one was open for 10% -> 27% of each run, Pallas kernels for 0% -> 0%
where the time goes in v1:
time: 237 us; the launch traced here: 236 us
  local copies, waits for them, and re-layouts  84.8 us (36%)
  starting transfers between devices  54.4 us (23%)
  blocking collectives  33.4 us (14%)
  matrix products  29.1 us (12%)
  waiting for transfers between devices  26.8 us (11%)
  other arithmetic  6.82 us (3%)
    all_to_all x1, blocking collectives, shards(): lax.all_to_all(shaped, ('row', 'col'), split_axis=0, concat_axis=2, tiled...  33.4 us
    ppermute x15, waiting for transfers between devices, exchange_directly(): lax.ppermute(sent, axis, [(i, (i + step) % size) for i in range(size)])  21.5 us
    ppermute x15, starting transfers between devices, exchange_directly(): lax.ppermute(sent, axis, [(i, (i + step) % size) for i in range(size)])  20.9 us
    dynamic_update_slice x16, local copies, waits for them, and re-layouts, exchange_directly(): result = lax.dynamic_update_slice_in_dim(result, theirs, source, axis=0)  20.3 us
    unnamed x26, local copies, waits for them, and re-layouts  18.3 us
    ppermute x4, starting transfers between devices, extended(): after = lax.ppermute(first, axis, down)  15.5 us
    dot_general x18, matrix products, convolve(): jnp.dot(cells, kernel[row_shift, col_shift], preferred_element_type=jnp.f...  9.57 us
    ppermute x4, starting transfers between devices, extended(): before = lax.ppermute(last, axis, up)  7.18 us
  transfers between devices with their start and end apart: 25, of which 6 were waited for; matrix products, arithmetic and copies ran while one was open for 27% of the time, Pallas kernels for 0%

profile of v1, /device:TPU:9, one launch (start us, length us, event | category | flops | bytes accessed | tf_op | source)
XLA Modules:
  0.0 235.8 jit_solution(16063494384297852893)
XLA Ops:
  0.0 3.6 %copy.41 = bf16[1,4,128,1280]{3,1,0,2:T(4,128)(2,1)} copy(bf16[1,4,128,1280]{3,2,1,0:T(8,128)(2,1)} %param.15) | data formatting | bytes 2621440 | tf_op args[4]
  3.6 6.6 %all-to-all-start.1 = ((bf16[1,4,128,1280]{3,1,0,2:T(4,128)(2,1)}), bf16[1,4,128,1280]{3,1,0,2:T(4,128)(2,1)}, u32[]{:S(2)}, u32[]{:S(2)}) async-start(bf16[1,4,128,1280]{3,1,0,2:T(4,128)(2,1)} %copy.41), calls=%async_computation.1 | async-start | bytes 2621440 | tf_op jit(solution)/shard_map/all_to_all | solution.py:114
  21.8 3.9 %fusion.33 = bf16[4,128,8,160]{1,3,2,0:T(8,128)(2,1)} fusion(bf16[4,128,8,160]{1,3,2,0:T(8,128)(2,1)} %bitcast.187, f32[4,8,128]{2,1,0:T(8,128)S(1)} %fusion.113, f32[4,8,128,128]{2,3,1,0:T(8,128)} %copy-done.4), kind=kOutput, calls=%fused_computation.59 | convolution fusion | flops 170528896 | bytes 4734976 | tf_op jit(solution)/shard_map/bhlm,bmhd->blhd/dot_general | solution.py:61
  25.7 4.3 %copy.37 = bf16[4,128,8,160]{3,2,1,0:T(8,128)(2,1)} copy(bf16[4,128,8,160]{1,3,2,0:T(8,128)(2,1)} %fusion.33) | data formatting | bytes 2621440 | tf_op jit(solution)/shard_map/convert_element_type | solution.py:63
  30.0 4.6 %reshape_reshape.12 = bf16[1,4,16,8,1280]{4,3,2,1,0:T(8,128)(2,1)} reshape(bf16[4,128,8,160]{3,2,1,0:T(8,128)(2,1)} %copy.37) | data formatting | bytes 2621440 | tf_op jit(solution)/shard_map/reshape;reshape | solution.py:16
  43.5 3.4 %copy.39 = bf16[1,4,128,1280]{3,1,0,2:T(4,128)(2,1)} copy(bf16[1,4,128,1280]{3,2,1,0:T(8,128)(2,1)} %param.14) | data formatting | bytes 2621440 | tf_op args[3]
  54.8 3.8 %collective-permute-start.8 = (bf16[1,1,4,8,1280]{4,3,0,2,1:T(8,128)(2,1)S(1)}, bf16[1,1,4,8,1280]{4,3,0,2,1:T(8,128)(2,1)}, u32[]{:S(2)}, u32[]{:S(2)}) collective-permute-start(bf16[1,1,4,8,1280]{4,3,0,2,1:T(8,128)(2,1)S(1)} %get-tuple-element.11), channel_id=1, source_target_pairs={{0,9},{1,10},{2,11},{3,12},{4,13},{5,14},{6,15},{7,0},{8,1},{9,2},... | collective-permute-start | bytes 245768 | tf_op jit(solution)/shard_map/ppermute | solution.py:32
  61.3 4.3 %all-to-all-start = ((bf16[1,4,128,1280]{3,1,0,2:T(4,128)(2,1)}), bf16[1,4,128,1280]{3,1,0,2:T(4,128)(2,1)}, u32[]{:S(2)}, u32[]{:S(2)}) async-start(bf16[1,4,128,1280]{3,1,0,2:T(4,128)(2,1)} %copy.39), calls=%async_computation | async-start | bytes 2621440 | tf_op jit(solution)/shard_map/all_to_all | solution.py:113
  68.7 3.2 %collective-permute-start.11 = (bf16[1,1,4,8,1280]{4,3,0,2,1:T(8,128)(2,1)S(1)}, bf16[1,1,4,8,1280]{4,3,0,2,1:T(8,128)(2,1)S(1)}, u32[]{:S(2)}, u32[]{:S(2)}) collective-permute-start(bf16[1,1,4,8,1280]{4,3,0,2,1:T(8,128)(2,1)S(1)} %get-tuple-element.8), channel_id=1, source_target_pairs={{0,12},{1,13},{2,14},{3,15},{4,0},{5,1},{6,2},{7,3},{8,4},{9,5},{1... | collective-permute-start | bytes 245768 | tf_op jit(solution)/shard_map/ppermute | solution.py:32
  79.8 19.3 %collective-permute-done.10 = bf16[1,1,4,8,1280]{4,3,0,2,1:T(8,128)(2,1)S(1)} collective-permute-done((bf16[1,1,4,8,1280]{4,3,0,2,1:T(8,128)(2,1)S(1)}, bf16[1,1,4,8,1280]{4,3,0,2,1:T(8,128)(2,1)S(1)}, u32[]{:S(2)}, u32[]{:S(2)}) %collective-permute-start.10) | collective-permute-done | bytes 81952 | tf_op jit(solution)/shard_map/ppermute | solution.py:32
  107.1 4.8 %reshape_reshape.13 = bf16[64,8,8,160]{3,2,1,0:T(8,128)(2,1)} reshape(bf16[16,1,4,8,1280]{4,3,2,0,1:T(8,128)(2,1)} %copy.38) | data formatting | bytes 2621440 | tf_op jit(solution)/shard_map/reshape;reshape | solution.py:120
  114.5 4.8 %reshape.107 = bf16[64,8,8,160]{3,2,1,0:T(8,128)(2,1)} reshape(bf16[16,1,4,8,1280]{4,3,2,0,1:T(8,128)(2,1)} %bitcast.167) | data formatting | bytes 2621440 | tf_op jit(solution)/shard_map/reshape | solution.py:120
  122.0 4.8 %reshape.106 = bf16[64,8,8,160]{3,2,1,0:T(8,128)(2,1)} reshape(bf16[16,1,4,8,1280]{4,3,2,0,1:T(8,128)(2,1)} %bitcast.168) | data formatting | bytes 2621440 | tf_op jit(solution)/shard_map/reshape | solution.py:120
  126.9 4.6 %fusion.26 = f32[8,8,64,64]{2,3,1,0:T(8,128)S(1)} fusion(bf16[64,8,8,160]{3,2,1,0:T(8,128)(2,1)} %reshape.107, bf16[64,8,8,160]{3,2,1,0:T(8,128)(2,1)} %reshape.106), kind=kOutput, calls=%fused_computation.41 | convolution fusion | flops 83886080 | bytes 3670016 | tf_op jit(solution)/shard_map/lbhd,mbhd->bhlm/dot_general | solution.py:67
  133.4 5.7 %convert_bitcast_fusion = bf16[64,8,8,160]{3,0,2,1:T(8,128)(2,1)} fusion(bf16[64,8,8,160]{3,2,1,0:T(8,128)(2,1)} %reshape_reshape.13, f32[8,8,64]{2,1,0:T(8,128)S(1)} %fusion.114, f32[8,8,64,64]{2,3,1,0:T(8,128)} %copy-done.3), kind=kOutput, calls=%fused_computation.45 | convolution fusion | flops 85594176 | bytes 3686400 | tf_op jit(solution)/shard_map/bhlm,mbhd->lbhd/dot_general | solution.py:71
  139.1 4.1 %copy.47 = bf16[64,8,8,160]{3,2,1,0:T(8,128)(2,1)} copy(bf16[64,8,8,160]{3,0,2,1:T(8,128)(2,1)} %convert_bitcast_fusion) | data formatting | bytes 2621440 | tf_op jit(solution)/shard_map/convert_element_type | solution.py:73
  143.1 4.6 %reshape.108 = bf16[512,1280]{1,0:T(8,128)(2,1)} reshape(bf16[64,8,8,160]{3,2,1,0:T(8,128)(2,1)} %copy.47) | data formatting | bytes 2621440 | tf_op jit(solution)/shard_map/reshape | solution.py:122
  150.6 33.4 %all_to_all.45 = bf16[16,4,8,1024]{3,2,1,0:T(8,128)(2,1)S(1)} all-to-all(bf16[16,4,8,1024]{3,2,1,0:T(8,128)(2,1)S(1)} %bitcast.188), channel_id=1, replica_groups=mesh['grp'=2,'row'=8,'col'=2] {'row','col'}, dimensions={0} | all-to-all | bytes 2097152 | tf_op jit(solution)/shard_map/all_to_all | solution.py:128
  192.3 3.6 %collective-permute-start.16 = (bf16[1,128,256]{2,1,0:T(8,128)(2,1)S(1)}, bf16[1,128,256]{2,1,0:T(8,128)(2,1)S(1)}, u32[]{:S(2)}, u32[]{:S(2)}) collective-permute-start(bf16[1,128,256]{2,1,0:T(8,128)(2,1)S(1)} %get-tuple-element.48), channel_id=1, source_target_pairs={{2,0},{4,2},{6,4},{8,6},{10,8},{12,10},{14,12},{3,1},{5,3},{7,5},{... | collective-permute-start | bytes 196616 | tf_op jit(solution)/shard_map/ppermute | solution.py:45
  198.9 3.5 %collective-permute-start.18 = (bf16[18,1,256]{2,1,0:T(2,128)(2,1)S(1)}, bf16[18,1,256]{2,1,0:T(2,128)(2,1)S(1)}, u32[]{:S(2)}, u32[]{:S(2)}) collective-permute-start(bf16[18,1,256]{2,1,0:T(2,128)(2,1)S(1)} %get-tuple-element.40), channel_id=1, source_target_pairs={{1,0},{3,2},{5,4},{7,6},{9,8},{11,10},{13,12},{15,14},{17,16},{19,... | collective-permute-start | bytes 27656 | tf_op jit(solution)/shard_map/ppermute | solution.py:45
  203.3 3.7 %pad_maximum_fusion.5 = (bf16[16,128,256]{2,1,0:T(8,128)(2,1)S(1)}, bf16[16,128,256]{2,1,0:T(8,128)(2,1)S(1)}, bf16[16,128,256]{2,1,0:T(8,128)(2,1)S(1)}, bf16[1...) fusion(bf16[18,128,256]{2,1,0:T(8,128)(2,1)S(1)} %constant_dynamic-update-slice_, ...), kind=kLoop, calls=%fused_computation.76 | loop fusion | flops 12582912 | bytes 7489536 | tf_op jit(solution)/shard_map/concatenate | solution.py:46
  212.0 4.6 %collective-permute-start.20 = (bf16[1,128,256]{2,1,0:T(8,128)(2,1)S(1)}, bf16[1,128,256]{2,1,0:T(8,128)(2,1)S(1)}, u32[]{:S(2)}, u32[]{:S(2)}) collective-permute-start(bf16[1,128,256]{2,1,0:T(8,128)(2,1)S(1)} %get-tuple-element.44), channel_id=1, source_target_pairs={{2,0},{4,2},{6,4},{8,6},{10,8},{12,10},{14,12},{3,1},{5,3},{7,5},{... | collective-permute-start | bytes 196616 | tf_op jit(solution)/shard_map/ppermute | solution.py:45
  218.8 3.9 %collective-permute-done.19 = bf16[1,128,256]{2,1,0:T(8,128)(2,1)S(1)} collective-permute-done((bf16[1,128,256]{2,1,0:T(8,128)(2,1)S(1)}, bf16[1,128,256]{2,1,0:T(8,128)(2,1)S(1)}, u32[]{:S(2)}, u32[]{:S(2)}) %collective-permute-start.19) | collective-permute-done | bytes 65568 | tf_op jit(solution)/shard_map/ppermute | solution.py:44
  224.0 3.8 %collective-permute-start.22 = (bf16[18,1,256]{2,1,0:T(2,128)(2,1)S(1)}, bf16[18,1,256]{2,1,0:T(2,128)(2,1)S(1)}, u32[]{:S(2)}, u32[]{:S(2)}) collective-permute-start(bf16[18,1,256]{2,1,0:T(2,128)(2,1)S(1)} %get-tuple-element.35), channel_id=1, source_target_pairs={{1,0},{3,2},{5,4},{7,6},{9,8},{11,10},{13,12},{15,14},{17,16},{19,... | collective-permute-start | bytes 27656 | tf_op jit(solution)/shard_map/ppermute | solution.py:45
  (120 shorter events, 88.4 us)
Async XLA Ops:
  3.6 57.8 %all-to-all-start.1 = ((bf16[1,4,128,1280]{3,1,0,2:T(4,128)(2,1)}), bf16[1,4,128,1280]{3,1,0,2:T(4,128)(2,1)}, u32[]{:S(2)}, u32[]{:S(2)}) async-start(bf16[1,4,128,1280]{3,1,0,2:T(4,128)(2,1)} %copy.41), calls=%async_computation.1 | async-start | bytes 2621440 | tf_op jit(solution)/shard_map/all_to_all | solution.py:114
  36.8 10.2 %collective-permute-start = (bf16[1,1,4,8,1280]{4,3,0,2,1:T(8,128)(2,1)}, bf16[1,1,4,8,1280]{4,3,0,2,1:T(8,128)(2,1)}, u32[]{:S(2)}, u32[]{:S(2)}) collective-permute-start(bf16[1,1,4,8,1280]{4,3,0,2,1:T(8,128)(2,1)} %get-tuple-element.19), channel_id=1, source_target_pairs={{0,1},{1,2},{2,3},{3,4},{4,5},{5,6},{6,7},{7,8},{8,9},{9,10},{10,1... | collective-permute-start | bytes 245768 | tf_op jit(solution)/shard_map/ppermute | solution.py:32
  38.2 11.4 %collective-permute-start.1 = (bf16[1,1,4,8,1280]{4,3,0,2,1:T(8,128)(2,1)}, bf16[1,1,4,8,1280]{4,3,0,2,1:T(8,128)(2,1)}, u32[]{:S(2)}, u32[]{:S(2)}) collective-permute-start(bf16[1,1,4,8,1280]{4,3,0,2,1:T(8,128)(2,1)} %get-tuple-element.18), channel_id=1, source_target_pairs={{0,2},{1,3},{2,4},{3,5},{4,6},{5,7},{6,8},{7,9},{8,10},{9,11},{10,... | collective-permute-start | bytes 245768 | tf_op jit(solution)/shard_map/ppermute | solution.py:32
  39.4 13.0 %collective-permute-start.2 = (bf16[1,1,4,8,1280]{4,3,0,2,1:T(8,128)(2,1)}, bf16[1,1,4,8,1280]{4,3,0,2,1:T(8,128)(2,1)}, u32[]{:S(2)}, u32[]{:S(2)}) collective-permute-start(bf16[1,1,4,8,1280]{4,3,0,2,1:T(8,128)(2,1)} %get-tuple-element.17), channel_id=1, source_target_pairs={{0,3},{1,4},{2,5},{3,6},{4,7},{5,8},{6,9},{7,10},{8,11},{9,12},{10... | collective-permute-start | bytes 245768 | tf_op jit(solution)/shard_map/ppermute | solution.py:32
  39.8 15.0 %collective-permute-start.3 = (bf16[1,1,4,8,1280]{4,3,0,2,1:T(8,128)(2,1)}, bf16[1,1,4,8,1280]{4,3,0,2,1:T(8,128)(2,1)}, u32[]{:S(2)}, u32[]{:S(2)}) collective-permute-start(bf16[1,1,4,8,1280]{4,3,0,2,1:T(8,128)(2,1)} %get-tuple-element.16), channel_id=1, source_target_pairs={{0,4},{1,5},{2,6},{3,7},{4,8},{5,9},{6,10},{7,11},{8,12},{9,13},{1... | collective-permute-start | bytes 245768 | tf_op jit(solution)/shard_map/ppermute | solution.py:32
  41.0 19.2 %collective-permute-start.4 = (bf16[1,1,4,8,1280]{4,3,0,2,1:T(8,128)(2,1)S(1)}, bf16[1,1,4,8,1280]{4,3,0,2,1:T(8,128)(2,1)}, u32[]{:S(2)}, u32[]{:S(2)}) collective-permute-start(bf16[1,1,4,8,1280]{4,3,0,2,1:T(8,128)(2,1)S(1)} %get-tuple-element.15), channel_id=1, source_target_pairs={{0,5},{1,6},{2,7},{3,8},{4,9},{5,10},{6,11},{7,12},{8,13},{9,14},{... | collective-permute-start | bytes 245768 | tf_op jit(solution)/shard_map/ppermute | solution.py:32
  46.9 20.3 %collective-permute-start.5 = (bf16[1,1,4,8,1280]{4,3,0,2,1:T(8,128)(2,1)S(1)}, bf16[1,1,4,8,1280]{4,3,0,2,1:T(8,128)(2,1)}, u32[]{:S(2)}, u32[]{:S(2)}) collective-permute-start(bf16[1,1,4,8,1280]{4,3,0,2,1:T(8,128)(2,1)S(1)} %get-tuple-element.14), channel_id=1, source_target_pairs={{0,6},{1,7},{2,8},{3,9},{4,10},{5,11},{6,12},{7,13},{8,14},{9,15},... | collective-permute-start | bytes 245768 | tf_op jit(solution)/shard_map/ppermute | solution.py:32
  49.6 19.1 %collective-permute-start.6 = (bf16[1,1,4,8,1280]{4,3,0,2,1:T(8,128)(2,1)S(1)}, bf16[1,1,4,8,1280]{4,3,0,2,1:T(8,128)(2,1)}, u32[]{:S(2)}, u32[]{:S(2)}) collective-permute-start(bf16[1,1,4,8,1280]{4,3,0,2,1:T(8,128)(2,1)S(1)} %get-tuple-element.13), channel_id=1, source_target_pairs={{0,7},{1,8},{2,9},{3,10},{4,11},{5,12},{6,13},{7,14},{8,15},{9,0},... | collective-permute-start | bytes 245768 | tf_op jit(solution)/shard_map/ppermute | solution.py:32
  52.4 21.1 %collective-permute-start.7 = (bf16[1,1,4,8,1280]{4,3,0,2,1:T(8,128)(2,1)S(1)}, bf16[1,1,4,8,1280]{4,3,0,2,1:T(8,128)(2,1)}, u32[]{:S(2)}, u32[]{:S(2)}) collective-permute-start(bf16[1,1,4,8,1280]{4,3,0,2,1:T(8,128)(2,1)S(1)} %get-tuple-element.12), channel_id=1, source_target_pairs={{0,8},{1,9},{2,10},{3,11},{4,12},{5,13},{6,14},{7,15},{8,0},{9,1},... | collective-permute-start | bytes 245768 | tf_op jit(solution)/shard_map/ppermute | solution.py:32
  54.8 21.6 %collective-permute-start.8 = (bf16[1,1,4,8,1280]{4,3,0,2,1:T(8,128)(2,1)S(1)}, bf16[1,1,4,8,1280]{4,3,0,2,1:T(8,128)(2,1)}, u32[]{:S(2)}, u32[]{:S(2)}) collective-permute-start(bf16[1,1,4,8,1280]{4,3,0,2,1:T(8,128)(2,1)S(1)} %get-tuple-element.11), channel_id=1, source_target_pairs={{0,9},{1,10},{2,11},{3,12},{4,13},{5,14},{6,15},{7,0},{8,1},{9,2},... | collective-permute-start | bytes 245768 | tf_op jit(solution)/shard_map/ppermute | solution.py:32
  60.2 19.0 %collective-permute-start.9 = (bf16[1,1,4,8,1280]{4,3,0,2,1:T(8,128)(2,1)S(1)}, bf16[1,1,4,8,1280]{4,3,0,2,1:T(8,128)(2,1)S(1)}, u32[]{:S(2)}, u32[]{:S(2)}) collective-permute-start(bf16[1,1,4,8,1280]{4,3,0,2,1:T(8,128)(2,1)S(1)} %get-tuple-element.10), channel_id=1, source_target_pairs={{0,10},{1,11},{2,12},{3,13},{4,14},{5,15},{6,0},{7,1},{8,2},{9,3},... | collective-permute-start | bytes 245768 | tf_op jit(solution)/shard_map/ppermute | solution.py:32
  61.3 58.1 %all-to-all-start = ((bf16[1,4,128,1280]{3,1,0,2:T(4,128)(2,1)}), bf16[1,4,128,1280]{3,1,0,2:T(4,128)(2,1)}, u32[]{:S(2)}, u32[]{:S(2)}) async-start(bf16[1,4,128,1280]{3,1,0,2:T(4,128)(2,1)} %copy.39), calls=%async_computation | async-start | bytes 2621440 | tf_op jit(solution)/shard_map/all_to_all | solution.py:113
  67.2 31.9 %collective-permute-start.10 = (bf16[1,1,4,8,1280]{4,3,0,2,1:T(8,128)(2,1)S(1)}, bf16[1,1,4,8,1280]{4,3,0,2,1:T(8,128)(2,1)S(1)}, u32[]{:S(2)}, u32[]{:S(2)}) collective-permute-start(bf16[1,1,4,8,1280]{4,3,0,2,1:T(8,128)(2,1)S(1)} %get-tuple-element.9), channel_id=1, source_target_pairs={{0,11},{1,12},{2,13},{3,14},{4,15},{5,0},{6,1},{7,2},{8,3},{9,4},{... | collective-permute-start | bytes 245768 | tf_op jit(solution)/shard_map/ppermute | solution.py:32
  68.7 31.2 %collective-permute-start.11 = (bf16[1,1,4,8,1280]{4,3,0,2,1:T(8,128)(2,1)S(1)}, bf16[1,1,4,8,1280]{4,3,0,2,1:T(8,128)(2,1)S(1)}, u32[]{:S(2)}, u32[]{:S(2)}) collective-permute-start(bf16[1,1,4,8,1280]{4,3,0,2,1:T(8,128)(2,1)S(1)} %get-tuple-element.8), channel_id=1, source_target_pairs={{0,12},{1,13},{2,14},{3,15},{4,0},{5,1},{6,2},{7,3},{8,4},{9,5},{1... | collective-permute-start | bytes 245768 | tf_op jit(solution)/shard_map/ppermute | solution.py:32
  73.4 29.1 %collective-permute-start.12 = (bf16[1,1,4,8,1280]{4,3,0,2,1:T(8,128)(2,1)S(1)}, bf16[1,1,4,8,1280]{4,3,0,2,1:T(8,128)(2,1)S(1)}, u32[]{:S(2)}, u32[]{:S(2)}) collective-permute-start(bf16[1,1,4,8,1280]{4,3,0,2,1:T(8,128)(2,1)S(1)} %get-tuple-element.7), channel_id=1, source_target_pairs={{0,13},{1,14},{2,15},{3,0},{4,1},{5,2},{6,3},{7,4},{8,5},{9,6},{10... | collective-permute-start | bytes 245768 | tf_op jit(solution)/shard_map/ppermute | solution.py:32
  76.4 26.8 %collective-permute-start.13 = (bf16[1,1,4,8,1280]{4,3,0,2,1:T(8,128)(2,1)S(1)}, bf16[1,1,4,8,1280]{4,3,0,2,1:T(8,128)(2,1)S(1)}, u32[]{:S(2)}, u32[]{:S(2)}) collective-permute-start(bf16[1,1,4,8,1280]{4,3,0,2,1:T(8,128)(2,1)S(1)} %get-tuple-element.6), channel_id=1, source_target_pairs={{0,14},{1,15},{2,0},{3,1},{4,2},{5,3},{6,4},{7,5},{8,6},{9,7},{10,... | collective-permute-start | bytes 245768 | tf_op jit(solution)/shard_map/ppermute | solution.py:32
  79.1 24.7 %collective-permute-start.14 = (bf16[1,1,4,8,1280]{4,3,0,2,1:T(8,128)(2,1)S(1)}, bf16[1,1,4,8,1280]{4,3,0,2,1:T(8,128)(2,1)S(1)}, u32[]{:S(2)}, u32[]{:S(2)}) collective-permute-start(bf16[1,1,4,8,1280]{4,3,0,2,1:T(8,128)(2,1)S(1)} %get-tuple-element.5), channel_id=1, source_target_pairs={{0,15},{1,0},{2,1},{3,2},{4,3},{5,4},{6,5},{7,6},{8,7},{9,8},{10,9... | collective-permute-start | bytes 245768 | tf_op jit(solution)/shard_map/ppermute | solution.py:32
  188.5 7.4 %collective-permute-start.15 = (bf16[1,128,256]{2,1,0:T(8,128)(2,1)S(1)}, bf16[1,128,256]{2,1,0:T(8,128)(2,1)S(1)}, u32[]{:S(2)}, u32[]{:S(2)}) collective-permute-start(bf16[1,128,256]{2,1,0:T(8,128)(2,1)S(1)} %get-tuple-element.49), channel_id=1, source_target_pairs={{0,2},{2,4},{4,6},{6,8},{8,10},{10,12},{12,14},{1,3},{3,5},{5,7},{... | collective-permute-start | bytes 196616 | tf_op jit(solution)/shard_map/ppermute | solution.py:44
  192.3 5.0 %collective-permute-start.16 = (bf16[1,128,256]{2,1,0:T(8,128)(2,1)S(1)}, bf16[1,128,256]{2,1,0:T(8,128)(2,1)S(1)}, u32[]{:S(2)}, u32[]{:S(2)}) collective-permute-start(bf16[1,128,256]{2,1,0:T(8,128)(2,1)S(1)} %get-tuple-element.48), channel_id=1, source_target_pairs={{2,0},{4,2},{6,4},{8,6},{10,8},{12,10},{14,12},{3,1},{5,3},{7,5},{... | collective-permute-start | bytes 196616 | tf_op jit(solution)/shard_map/ppermute | solution.py:45
  197.6 5.7 %collective-permute-start.17 = (bf16[18,1,256]{2,1,0:T(2,128)(2,1)S(1)}, bf16[18,1,256]{2,1,0:T(2,128)(2,1)S(1)}, u32[]{:S(2)}, u32[]{:S(2)}) collective-permute-start(bf16[18,1,256]{2,1,0:T(2,128)(2,1)S(1)} %get-tuple-element.39), channel_id=1, source_target_pairs={{0,1},{2,3},{4,5},{6,7},{8,9},{10,11},{12,13},{14,15},{16,17},{18,... | collective-permute-start | bytes 27656 | tf_op jit(solution)/shard_map/ppermute | solution.py:44
  212.0 6.7 %collective-permute-start.20 = (bf16[1,128,256]{2,1,0:T(8,128)(2,1)S(1)}, bf16[1,128,256]{2,1,0:T(8,128)(2,1)S(1)}, u32[]{:S(2)}, u32[]{:S(2)}) collective-permute-start(bf16[1,128,256]{2,1,0:T(8,128)(2,1)S(1)} %get-tuple-element.44), channel_id=1, source_target_pairs={{2,0},{4,2},{6,4},{8,6},{10,8},{12,10},{14,12},{3,1},{5,3},{7,5},{... | collective-permute-start | bytes 196616 | tf_op jit(solution)/shard_map/ppermute | solution.py:45
  216.6 6.0 %collective-permute-start.19 = (bf16[1,128,256]{2,1,0:T(8,128)(2,1)S(1)}, bf16[1,128,256]{2,1,0:T(8,128)(2,1)S(1)}, u32[]{:S(2)}, u32[]{:S(2)}) collective-permute-start(bf16[1,128,256]{2,1,0:T(8,128)(2,1)S(1)} %get-tuple-element.43), channel_id=1, source_target_pairs={{0,2},{2,4},{4,6},{6,8},{8,10},{10,12},{12,14},{1,3},{3,5},{5,7},{... | collective-permute-start | bytes 196616 | tf_op jit(solution)/shard_map/ppermute | solution.py:44
  222.7 5.7 %collective-permute-start.21 = (bf16[18,1,256]{2,1,0:T(2,128)(2,1)S(1)}, bf16[18,1,256]{2,1,0:T(2,128)(2,1)S(1)}, u32[]{:S(2)}, u32[]{:S(2)}) collective-permute-start(bf16[18,1,256]{2,1,0:T(2,128)(2,1)S(1)} %get-tuple-element.34), channel_id=1, source_target_pairs={{0,1},{2,3},{4,5},{6,7},{8,9},{10,11},{12,13},{14,15},{16,17},{18,... | collective-permute-start | bytes 27656 | tf_op jit(solution)/shard_map/ppermute | solution.py:44
  224.0 4.5 %collective-permute-start.22 = (bf16[18,1,256]{2,1,0:T(2,128)(2,1)S(1)}, bf16[18,1,256]{2,1,0:T(2,128)(2,1)S(1)}, u32[]{:S(2)}, u32[]{:S(2)}) collective-permute-start(bf16[18,1,256]{2,1,0:T(2,128)(2,1)S(1)} %get-tuple-element.35), channel_id=1, source_target_pairs={{1,0},{3,2},{5,4},{7,6},{9,8},{11,10},{13,12},{15,14},{17,16},{19,... | collective-permute-start | bytes 27656 | tf_op jit(solution)/shard_map/ppermute | solution.py:45
  (11 other events, 181.7 us)
